TPU v7x, 32 devices: a whole 2x2x4 slice. The times are simulated.
32 devices in a mesh: req: 8 (over z, y), tp: 4 (over x, core).
Axes of the slice: x: 2, y: 2, z: 4, core: 2. Of those that a mesh axis runs over, the one named last changes fastest.
Arguments:
- tokens: bfloat16 [4096, 2048], P('req')
- token_request_number: int32 [8, 512], P('req'), may hold values from 0 to 7, never falling along the last dimension, each value on 1 to 256 neighbouring positions
- request_adapter_position: int32 [8, 8], P('req'), may hold values from 0 to 15
- adapters_in_use: int32 [16], replicated, may hold values from 0 to 15, as said below
- adapter_storage_slot: int32 [16], replicated, may hold values from 0 to 15, each once
- input_norm_gain: bfloat16 [2048], replicated, may hold values from 0.5 to 1.5
- query_weight: bfloat16 [2048, 2048], P('req', 'tp')
- key_weight: bfloat16 [2048, 2048], P('req', 'tp')
- value_weight: bfloat16 [2048, 2048], P('req', 'tp'), may hold values from -0.125 to 0.125
- output_weight: bfloat16 [2048, 2048], P('tp', 'req'), may hold values from -0.125 to 0.125
- adapter_down_weight: bfloat16 [16, 2, 16, 2048], P('req'), may hold values from -0.125 to 0.125
- adapter_up_weight: bfloat16 [16, 2, 16, 2048], P('req', None, None, 'tp'), may hold values from -0.75 to 0.75
Outputs:
- layer_out: bfloat16 [4096, 2048], P('req', 'tp')
Inputs may be any that keep to these rules, and one draw needn't show every extreme that they name: `adapters_in_use`: 16 different adapter numbers; 0 and 15 are always among them. `token_request_number`: the 512 tokens of each index of req form exactly 8 requests in order, each of 1 to 256 tokens, and one of exactly 256.
All inputs are finite; a program needn't handle non-finite values.
Results may differ from a plain program's by a relative error of at most 0.01.
Values may be sent and summed in bfloat16 or wider, within the bound.
A program may use at most 64 MiB of HBM per device.

v0:
```python
import jax
import jax.numpy as jnp
from jax import lax
from jax.sharding import PartitionSpec as P

HEAD_WIDTH = 64
norm_eps = 1e-05
rope_base = 130000.0
adapter_scale = 2.0


def spread_2(value, axis, root):
    mine = lax.axis_index(axis) == root
    return lax.psum(jnp.where(mine, value, jnp.zeros_like(value)), axis)


def positions_of(segment):
    ordinal = jnp.arange(segment.shape[0], dtype=jnp.int32)
    starts = jnp.concatenate([jnp.ones((1,), jnp.bool_), segment[1:] != segment[:-1]])
    segment_start = lax.cummax(jnp.where(starts, ordinal, jnp.zeros_like(ordinal)), axis=0)
    return ordinal - segment_start


def apply_rotation(values, token_positions):
    half_dim = HEAD_WIDTH // 2
    frequency = rope_base ** (-(jnp.arange(half_dim, dtype=jnp.float32) * 2.0 / HEAD_WIDTH))
    angles = token_positions.astype(jnp.float32)[:, None] * frequency[None, :]
    cosine = jnp.cos(angles)[:, None, :]
    sine_part = jnp.sin(angles)[:, None, :]
    first_half = values[..., :half_dim]
    second_half = values[..., half_dim:]
    return jnp.concatenate(
        [
            first_half * cosine - second_half * sine_part,
            second_half * cosine + first_half * sine_part,
        ],
        axis=-1,
    )


def attend(query_per_head, key_heads, value_per_head, segment):
    scores = (
        jnp.einsum("qhd,khd->hqk", query_per_head, key_heads, preferred_element_type=jnp.float32)
        * 0.125
    )
    ordinal = jnp.arange(segment.shape[0], dtype=jnp.int32)
    allowed = (segment[:, None] == segment[None, :]) & (ordinal[None, :] <= ordinal[:, None])
    scores = jnp.where(allowed[None], scores, jnp.float32(-1e30))
    row_peak = jnp.max(scores, axis=-1, keepdims=True)
    exponent = jnp.where(allowed[None], jnp.exp(scores - row_peak), jnp.float32(0.0))
    weights = (exponent / jnp.sum(exponent, axis=-1, keepdims=True)).astype(jnp.bfloat16)
    return jnp.einsum(
        "hqk,khd->qhd", weights, value_per_head, preferred_element_type=jnp.float32
    ).astype(jnp.bfloat16)


def local(
    tokens,
    token_request_number,
    request_adapter_position,
    adapters_in_use,
    adapter_storage_slot,
    input_norm_gain,
    query_weight,
    key_weight,
    value_weight,
    output_weight,
    adapter_down_weight,
    adapter_up_weight,
):
    row_total, model_width = tokens.shape
    local_width = query_weight.shape[1]
    reduced_rows = adapter_down_weight.shape[2]
    active_count = adapters_in_use.shape[0]
    slot_total = adapter_down_weight.shape[0]
    segment = token_request_number[0]
    request_adapters = request_adapter_position[0]
    storage_slots = jnp.take(adapter_storage_slot, adapters_in_use, axis=0)
    stored_weight = jnp.concatenate([adapter_down_weight, adapter_up_weight], axis=3)

    def fetch_one(active_index, fetched):
        home = storage_slots[active_index]
        own_slot = lax.dynamic_index_in_dim(stored_weight, home % slot_total, 0, keepdims=False)
        received = spread_2(own_slot, "req", home // slot_total)
        return lax.dynamic_update_index_in_dim(fetched, received, active_index, 0)

    fetched = lax.fori_loop(
        0,
        active_count,
        fetch_one,
        jnp.zeros((active_count,) + stored_weight.shape[1:], jnp.bfloat16),
    )
    fetch_down = fetched[..., :model_width]
    fetch_up = fetched[..., model_width:]
    floats = tokens.astype(jnp.float32)
    normed = (
        floats
        * lax.rsqrt(jnp.mean(floats * floats, axis=-1, keepdims=True) + norm_eps)
        * input_norm_gain.astype(jnp.float32)
    ).astype(jnp.bfloat16)
    query_plain = jnp.dot(
        normed,
        lax.all_gather(query_weight, "req", axis=0, tiled=True),
        preferred_element_type=jnp.float32,
    )
    key_base = jnp.dot(
        normed,
        lax.all_gather(key_weight, "req", axis=0, tiled=True),
        preferred_element_type=jnp.float32,
    )
    value_plain = jnp.dot(
        normed,
        lax.all_gather(value_weight, "req", axis=0, tiled=True),
        preferred_element_type=jnp.float32,
    )
    request_total = request_adapters.shape[0]
    member = segment[:, None] == jnp.arange(request_total, dtype=jnp.int32)[None, :]
    token_adapter = jnp.sum(
        jnp.where(member, request_adapters[None, :], jnp.zeros_like(request_adapters)[None, :]),
        axis=1,
    )
    select = token_adapter[:, None] == jnp.arange(active_count, dtype=jnp.int32)[None, :]
    shrunk_all = lax.dot_general(
        normed,
        fetch_down.reshape(active_count * 2 * reduced_rows, model_width),
        (((1,), (1,)), ((), ())),
        preferred_element_type=jnp.float32,
    )
    shrunk_all = shrunk_all.reshape(row_total, active_count, 2, reduced_rows)
    shrunk = jnp.sum(
        jnp.where(select[:, :, None, None], shrunk_all, jnp.float32(0.0)), axis=1
    ).astype(jnp.bfloat16)
    spread = jnp.where(select[:, :, None, None], shrunk[:, None, :, :], jnp.zeros((), jnp.bfloat16))
    query_change = jnp.dot(
        spread[:, :, 0, :].reshape(row_total, active_count * reduced_rows),
        fetch_up[:, 0].reshape(active_count * reduced_rows, local_width),
        preferred_element_type=jnp.float32,
    )
    value_change = jnp.dot(
        spread[:, :, 1, :].reshape(row_total, active_count * reduced_rows),
        fetch_up[:, 1].reshape(active_count * reduced_rows, local_width),
        preferred_element_type=jnp.float32,
    )
    head_total = local_width // HEAD_WIDTH
    token_positions = positions_of(segment)
    query_per_head = apply_rotation(
        (query_plain + adapter_scale * query_change).reshape(row_total, head_total, HEAD_WIDTH),
        token_positions,
    ).astype(jnp.bfloat16)
    key_heads = apply_rotation(
        key_base.reshape(row_total, head_total, HEAD_WIDTH), token_positions
    ).astype(jnp.bfloat16)
    value_per_head = (
        (value_plain + adapter_scale * value_change)
        .astype(jnp.bfloat16)
        .reshape(row_total, head_total, HEAD_WIDTH)
    )
    attended = attend(query_per_head, key_heads, value_per_head, segment).reshape(
        row_total, local_width
    )
    partial_out = jnp.dot(
        attended,
        lax.all_gather(output_weight, "req", axis=1, tiled=True),
        preferred_element_type=jnp.float32,
    )
    summed = lax.psum_scatter(
        partial_out.astype(jnp.bfloat16), "tp", scatter_dimension=1, tiled=True
    ).astype(jnp.float32)
    share_width = summed.shape[1]
    residual_part = lax.dynamic_slice_in_dim(
        tokens, lax.axis_index("tp") * share_width, share_width, 1
    )
    return (summed + residual_part.astype(jnp.float32)).astype(jnp.bfloat16)


def solution(mesh):
    in_specs = (
        P("req", None),
        P("req", None),
        P("req", None),
        P(),
        P(),
        P(),
        P("req", "tp"),
        P("req", "tp"),
        P("req", "tp"),
        P("tp", "req"),
        P("req", None, None, None),
        P("req", None, None, "tp"),
    )
    out_specs = P("req", "tp")
    return jax.shard_map(local, mesh=mesh, in_specs=in_specs, out_specs=out_specs, check_vma=False)
```

profile of v0, /device:TPU:0, one launch (start us, length us, event | category | flops | bytes accessed | tf_op | source)
XLA Modules:
  0.0 1461.1 jit_solution(2238570392540167822)
XLA Ops:
  10.6 1205.2 %while.15 = (s32[]{:T(128)}, bf16[16,2,16,2560]{3,2,1,0:T(8,128)(2,1)}, s32[16]{0:T(128)S(1)}, bf16[2,2,16,2560]{3,2,1,0:T(8,128)(2,1)S(1)}, s32[]{:T(128)}, /*i...) while((s32[]{:T(128)}, bf16[16,2,16,2560]{3,2,1,0:T(8,128)(2,1)}, s32[16]{0:T(128)S(1)}, ...), condition=%wide.region_4.5_spmd, body=%wide.region_2.4_spmd.sunk | while | flops 163868 | bytes 1638832 | solution.py:87
  14.5 72.8 %all-reduce.2.cloned.1.call-done = bf16[1,2,16,2560]{3,2,1,0:T(8,128)(2,1)} async-done(((bf16[1,2,16,2560]{3,2,1,0:T(8,128)(2,1)}), bf16[1,2,16,2560]{3,2,1,0:T(8,128)(2,1)}) %all-reduce.2.cloned.1.call-update) | async-done | bytes 163856 | tf_op jit(solution)/shard_map/while/body/eval_jaxpr/psum | solution.py:14
  87.3 1.6 constant_dynamic-update-slice_fusion.2
  92.8 69.8 %all-reduce.2.cloned.1.call-done = bf16[1,2,16,2560]{3,2,1,0:T(8,128)(2,1)} async-done(((bf16[1,2,16,2560]{3,2,1,0:T(8,128)(2,1)}), bf16[1,2,16,2560]{3,2,1,0:T(8,128)(2,1)}) %all-reduce.2.cloned.1.call-update) | async-done | bytes 163856 | tf_op jit(solution)/shard_map/while/body/eval_jaxpr/psum | solution.py:14
  162.6 1.6 constant_dynamic-update-slice_fusion.2
  168.1 69.8 %all-reduce.2.cloned.1.call-done = bf16[1,2,16,2560]{3,2,1,0:T(8,128)(2,1)} async-done(((bf16[1,2,16,2560]{3,2,1,0:T(8,128)(2,1)}), bf16[1,2,16,2560]{3,2,1,0:T(8,128)(2,1)}) %all-reduce.2.cloned.1.call-update) | async-done | bytes 163856 | tf_op jit(solution)/shard_map/while/body/eval_jaxpr/psum | solution.py:14
  237.8 1.6 constant_dynamic-update-slice_fusion.2
  243.3 69.5 %all-reduce.2.cloned.1.call-done = bf16[1,2,16,2560]{3,2,1,0:T(8,128)(2,1)} async-done(((bf16[1,2,16,2560]{3,2,1,0:T(8,128)(2,1)}), bf16[1,2,16,2560]{3,2,1,0:T(8,128)(2,1)}) %all-reduce.2.cloned.1.call-update) | async-done | bytes 163856 | tf_op jit(solution)/shard_map/while/body/eval_jaxpr/psum | solution.py:14
  312.8 1.6 constant_dynamic-update-slice_fusion.2
  318.3 69.5 %all-reduce.2.cloned.1.call-done = bf16[1,2,16,2560]{3,2,1,0:T(8,128)(2,1)} async-done(((bf16[1,2,16,2560]{3,2,1,0:T(8,128)(2,1)}), bf16[1,2,16,2560]{3,2,1,0:T(8,128)(2,1)}) %all-reduce.2.cloned.1.call-update) | async-done | bytes 163856 | tf_op jit(solution)/shard_map/while/body/eval_jaxpr/psum | solution.py:14
  387.8 1.6 constant_dynamic-update-slice_fusion.2
  393.3 69.5 %all-reduce.2.cloned.1.call-done = bf16[1,2,16,2560]{3,2,1,0:T(8,128)(2,1)} async-done(((bf16[1,2,16,2560]{3,2,1,0:T(8,128)(2,1)}), bf16[1,2,16,2560]{3,2,1,0:T(8,128)(2,1)}) %all-reduce.2.cloned.1.call-update) | async-done | bytes 163856 | tf_op jit(solution)/shard_map/while/body/eval_jaxpr/psum | solution.py:14
  462.8 1.6 constant_dynamic-update-slice_fusion.2
  468.3 69.8 %all-reduce.2.cloned.1.call-done = bf16[1,2,16,2560]{3,2,1,0:T(8,128)(2,1)} async-done(((bf16[1,2,16,2560]{3,2,1,0:T(8,128)(2,1)}), bf16[1,2,16,2560]{3,2,1,0:T(8,128)(2,1)}) %all-reduce.2.cloned.1.call-update) | async-done | bytes 163856 | tf_op jit(solution)/shard_map/while/body/eval_jaxpr/psum | solution.py:14
  538.1 1.6 constant_dynamic-update-slice_fusion.2
  543.6 69.8 %all-reduce.2.cloned.1.call-done = bf16[1,2,16,2560]{3,2,1,0:T(8,128)(2,1)} async-done(((bf16[1,2,16,2560]{3,2,1,0:T(8,128)(2,1)}), bf16[1,2,16,2560]{3,2,1,0:T(8,128)(2,1)}) %all-reduce.2.cloned.1.call-update) | async-done | bytes 163856 | tf_op jit(solution)/shard_map/while/body/eval_jaxpr/psum | solution.py:14
  613.4 1.6 constant_dynamic-update-slice_fusion.2
  618.9 69.8 %all-reduce.2.cloned.1.call-done = bf16[1,2,16,2560]{3,2,1,0:T(8,128)(2,1)} async-done(((bf16[1,2,16,2560]{3,2,1,0:T(8,128)(2,1)}), bf16[1,2,16,2560]{3,2,1,0:T(8,128)(2,1)}) %all-reduce.2.cloned.1.call-update) | async-done | bytes 163856 | tf_op jit(solution)/shard_map/while/body/eval_jaxpr/psum | solution.py:14
  688.7 1.6 constant_dynamic-update-slice_fusion.2
  694.2 69.5 %all-reduce.2.cloned.1.call-done = bf16[1,2,16,2560]{3,2,1,0:T(8,128)(2,1)} async-done(((bf16[1,2,16,2560]{3,2,1,0:T(8,128)(2,1)}), bf16[1,2,16,2560]{3,2,1,0:T(8,128)(2,1)}) %all-reduce.2.cloned.1.call-update) | async-done | bytes 163856 | tf_op jit(solution)/shard_map/while/body/eval_jaxpr/psum | solution.py:14
  763.6 1.6 constant_dynamic-update-slice_fusion.2
  769.1 69.8 %all-reduce.2.cloned.1.call-done = bf16[1,2,16,2560]{3,2,1,0:T(8,128)(2,1)} async-done(((bf16[1,2,16,2560]{3,2,1,0:T(8,128)(2,1)}), bf16[1,2,16,2560]{3,2,1,0:T(8,128)(2,1)}) %all-reduce.2.cloned.1.call-update) | async-done | bytes 163856 | tf_op jit(solution)/shard_map/while/body/eval_jaxpr/psum | solution.py:14
  838.9 1.6 constant_dynamic-update-slice_fusion.2
  844.4 69.5 %all-reduce.2.cloned.1.call-done = bf16[1,2,16,2560]{3,2,1,0:T(8,128)(2,1)} async-done(((bf16[1,2,16,2560]{3,2,1,0:T(8,128)(2,1)}), bf16[1,2,16,2560]{3,2,1,0:T(8,128)(2,1)}) %all-reduce.2.cloned.1.call-update) | async-done | bytes 163856 | tf_op jit(solution)/shard_map/while/body/eval_jaxpr/psum | solution.py:14
  913.9 1.6 constant_dynamic-update-slice_fusion.2
  919.4 69.8 %all-reduce.2.cloned.1.call-done = bf16[1,2,16,2560]{3,2,1,0:T(8,128)(2,1)} async-done(((bf16[1,2,16,2560]{3,2,1,0:T(8,128)(2,1)}), bf16[1,2,16,2560]{3,2,1,0:T(8,128)(2,1)}) %all-reduce.2.cloned.1.call-update) | async-done | bytes 163856 | tf_op jit(solution)/shard_map/while/body/eval_jaxpr/psum | solution.py:14
  989.2 1.6 constant_dynamic-update-slice_fusion.2
  994.7 69.5 %all-reduce.2.cloned.1.call-done = bf16[1,2,16,2560]{3,2,1,0:T(8,128)(2,1)} async-done(((bf16[1,2,16,2560]{3,2,1,0:T(8,128)(2,1)}), bf16[1,2,16,2560]{3,2,1,0:T(8,128)(2,1)}) %all-reduce.2.cloned.1.call-update) | async-done | bytes 163856 | tf_op jit(solution)/shard_map/while/body/eval_jaxpr/psum | solution.py:14
  1064.2 1.6 constant_dynamic-update-slice_fusion.2
  1069.7 69.5 %all-reduce.2.cloned.1.call-done = bf16[1,2,16,2560]{3,2,1,0:T(8,128)(2,1)} async-done(((bf16[1,2,16,2560]{3,2,1,0:T(8,128)(2,1)}), bf16[1,2,16,2560]{3,2,1,0:T(8,128)(2,1)}) %all-reduce.2.cloned.1.call-update) | async-done | bytes 163856 | tf_op jit(solution)/shard_map/while/body/eval_jaxpr/psum | solution.py:14
  1139.1 1.6 constant_dynamic-update-slice_fusion.2
  1144.6 69.5 %all-reduce.2.cloned.1.call-done = bf16[1,2,16,2560]{3,2,1,0:T(8,128)(2,1)} async-done(((bf16[1,2,16,2560]{3,2,1,0:T(8,128)(2,1)}), bf16[1,2,16,2560]{3,2,1,0:T(8,128)(2,1)}) %all-reduce.2.cloned.1.call-update) | async-done | bytes 163856 | tf_op jit(solution)/shard_map/while/body/eval_jaxpr/psum | solution.py:14
  1214.1 1.6 constant_dynamic-update-slice_fusion.2
  1219.9 3.0 fusion.23
  1223.9 43.4 %all-gather.5.cloned.1.call-done = bf16[2048,512]{1,0:T(8,128)(2,1)} async-done(((bf16[256,512]{1,0:T(8,128)(2,1)}), bf16[2048,512]{1,0:T(8,128)(2,1)}) %all-gather.5.cloned.1.call-update) | async-done | bytes 2097168 | tf_op jit(solution)/shard_map/all_gather | solution.py:113
  1267.3 3.0 fusion.44
  1270.4 2.1 fusion.22
  1272.5 44.6 %all-gather.7.cloned.1.call-done = bf16[2048,512]{1,0:T(8,128)(2,1)} async-done(((bf16[256,512]{1,0:T(8,128)(2,1)}), bf16[2048,512]{1,0:T(8,128)(2,1)}) %all-gather.7.cloned.1.call-update) | async-done | bytes 2097168 | tf_op jit(solution)/shard_map/all_gather | solution.py:103
  1317.1 3.1 fusion.41
  1320.2 1.3 fusion.20
  1321.5 45.3 %all-gather.9.cloned.1.call-done = bf16[2048,512]{1,0:T(8,128)(2,1)} async-done(((bf16[256,512]{1,0:T(8,128)(2,1)}), bf16[2048,512]{1,0:T(8,128)(2,1)}) %all-gather.9.cloned.1.call-update) | async-done | bytes 2097168 | tf_op jit(solution)/shard_map/all_gather | solution.py:108
  1366.8 3.0 fusion.39
  1371.1 8.1 fusion.46
  1379.2 4.3 fusion.21
  1383.5 34.4 %all-gather.11.cloned.1.call-done = bf16[512,2048]{1,0:T(8,128)(2,1)} async-done(((bf16[512,256]{1,0:T(8,128)(2,1)}), bf16[512,2048]{1,0:T(8,128)(2,1)}) %all-gather.11.cloned.1.call-update) | async-done | bytes 2097168 | tf_op jit(solution)/shard_map/all_gather | solution.py:163
  1417.9 4.2 convolution_convert_fusion
  1422.2 29.6 %reduce-scatter.2.cloned.1.call-done = bf16[512,512]{1,0:T(8,128)(2,1)} async-done(((bf16[512,2048]{1,0:T(8,128)(2,1)}), bf16[512,512]{1,0:T(8,128)(2,1)}) %reduce-scatter.2.cloned.1.call-update) | async-done | bytes 524304 | tf_op jit(solution)/shard_map/reduce_scatter | solution.py:166
  1451.8 2.0 add_convert_fusion
  (113 shorter events, 30.2 us)
Async XLA Ops:
  7.4 0.7 copy-start
  9.4 1208.9 %copy-start.1 = (bf16[512,2048]{1,0:T(8,128)(2,1)S(1)}, bf16[512,2048]{1,0:T(8,128)(2,1)}, u32[]{:S(2)}) copy-start(bf16[512,2048]{1,0:T(8,128)(2,1)} %param.14) | copy-start | bytes 6291460
  10.5 1207.7 %copy-start.6 = (bf16[2048]{0:T(1024)(128)(2,1)S(1)}, bf16[2048]{0:T(1024)(128)(2,1)}, u32[]{:S(2)}) copy-start(bf16[2048]{0:T(1024)(128)(2,1)} %param.19) | copy-start | bytes 12292
  10.6 76.7 %all-reduce.2.cloned.1.call-start = ((), (), s32[]{:S(2)}) async-start(), calls=%async_computation.6 | async-start | bytes 327680 | tf_op jit(solution)/shard_map/while/body/eval_jaxpr/psum | solution.py:14
  88.9 73.7 %all-reduce.2.cloned.1.call-start = ((), (), s32[]{:S(2)}) async-start(), calls=%async_computation.6 | async-start | bytes 327680 | tf_op jit(solution)/shard_map/while/body/eval_jaxpr/psum | solution.py:14
  164.2 73.7 %all-reduce.2.cloned.1.call-start = ((), (), s32[]{:S(2)}) async-start(), calls=%async_computation.6 | async-start | bytes 327680 | tf_op jit(solution)/shard_map/while/body/eval_jaxpr/psum | solution.py:14
  239.4 73.4 %all-reduce.2.cloned.1.call-start = ((), (), s32[]{:S(2)}) async-start(), calls=%async_computation.6 | async-start | bytes 327680 | tf_op jit(solution)/shard_map/while/body/eval_jaxpr/psum | solution.py:14
  314.4 73.4 %all-reduce.2.cloned.1.call-start = ((), (), s32[]{:S(2)}) async-start(), calls=%async_computation.6 | async-start | bytes 327680 | tf_op jit(solution)/shard_map/while/body/eval_jaxpr/psum | solution.py:14
  389.4 73.4 %all-reduce.2.cloned.1.call-start = ((), (), s32[]{:S(2)}) async-start(), calls=%async_computation.6 | async-start | bytes 327680 | tf_op jit(solution)/shard_map/while/body/eval_jaxpr/psum | solution.py:14
  464.4 73.7 %all-reduce.2.cloned.1.call-start = ((), (), s32[]{:S(2)}) async-start(), calls=%async_computation.6 | async-start | bytes 327680 | tf_op jit(solution)/shard_map/while/body/eval_jaxpr/psum | solution.py:14
  539.7 73.7 %all-reduce.2.cloned.1.call-start = ((), (), s32[]{:S(2)}) async-start(), calls=%async_computation.6 | async-start | bytes 327680 | tf_op jit(solution)/shard_map/while/body/eval_jaxpr/psum | solution.py:14
  615.0 73.7 %all-reduce.2.cloned.1.call-start = ((), (), s32[]{:S(2)}) async-start(), calls=%async_computation.6 | async-start | bytes 327680 | tf_op jit(solution)/shard_map/while/body/eval_jaxpr/psum | solution.py:14
  690.2 73.4 %all-reduce.2.cloned.1.call-start = ((), (), s32[]{:S(2)}) async-start(), calls=%async_computation.6 | async-start | bytes 327680 | tf_op jit(solution)/shard_map/while/body/eval_jaxpr/psum | solution.py:14
  765.2 73.7 %all-reduce.2.cloned.1.call-start = ((), (), s32[]{:S(2)}) async-start(), calls=%async_computation.6 | async-start | bytes 327680 | tf_op jit(solution)/shard_map/while/body/eval_jaxpr/psum | solution.py:14
  840.5 73.4 %all-reduce.2.cloned.1.call-start = ((), (), s32[]{:S(2)}) async-start(), calls=%async_computation.6 | async-start | bytes 327680 | tf_op jit(solution)/shard_map/while/body/eval_jaxpr/psum | solution.py:14
  915.5 73.7 %all-reduce.2.cloned.1.call-start = ((), (), s32[]{:S(2)}) async-start(), calls=%async_computation.6 | async-start | bytes 327680 | tf_op jit(solution)/shard_map/while/body/eval_jaxpr/psum | solution.py:14
  990.8 73.4 %all-reduce.2.cloned.1.call-start = ((), (), s32[]{:S(2)}) async-start(), calls=%async_computation.6 | async-start | bytes 327680 | tf_op jit(solution)/shard_map/while/body/eval_jaxpr/psum | solution.py:14
  1065.8 73.4 %all-reduce.2.cloned.1.call-start = ((), (), s32[]{:S(2)}) async-start(), calls=%async_computation.6 | async-start | bytes 327680 | tf_op jit(solution)/shard_map/while/body/eval_jaxpr/psum | solution.py:14
  1140.7 73.4 %all-reduce.2.cloned.1.call-start = ((), (), s32[]{:S(2)}) async-start(), calls=%async_computation.6 | async-start | bytes 327680 | tf_op jit(solution)/shard_map/while/body/eval_jaxpr/psum | solution.py:14
  1215.7 3.1 copy-start.5
  1215.7 4.1 copy-start.7
  1215.7 51.6 %all-gather.5.cloned.1.call-start = ((), (), s32[]{:S(2)}) async-start(), calls=%async_computation.1 | async-start | bytes 2359296 | tf_op jit(solution)/shard_map/all_gather | solution.py:113
  1216.3 100.8 %all-gather.7.cloned.1.call-start = ((), (), s32[]{:S(2)}) async-start(), calls=%async_computation.2 | async-start | bytes 2359296 | tf_op jit(solution)/shard_map/all_gather | solution.py:103
  1216.9 149.9 %all-gather.9.cloned.1.call-start = ((), (), s32[]{:S(2)}) async-start(), calls=%async_computation.3 | async-start | bytes 2359296 | tf_op jit(solution)/shard_map/all_gather | solution.py:108
  1217.5 200.4 %all-gather.11.cloned.1.call-start = ((), (), s32[]{:S(2)}) async-start(), calls=%async_computation.4 | async-start | bytes 2359296 | tf_op jit(solution)/shard_map/all_gather | solution.py:163
  1218.2 233.6 %reduce-scatter.2.cloned.1.call-start = ((), (), s32[]{:S(2)}) async-start(), calls=%async_computation.5 | async-start | bytes 2621440 | tf_op jit(solution)/shard_map/reduce_scatter | solution.py:166
  1222.9 47.4 %copy-start.2 = (bf16[512,16,2,16]{0,3,2,1:T(8,128)(2,1)}, bf16[512,16,2,16]{0,3,2,1:T(8,128)(2,1)S(1)}, u32[]{:S(2)}) copy-start(bf16[512,16,2,16]{0,3,2,1:T(8,128)(2,1)S(1)} %broadcast_select_fusion) | copy-start | bytes 1572868
  1317.0 3.1 copy-start.3
  1371.1 8.1 copy-start.4
Sparse Core Ops, SparseCore 0:
  15.1 72.1 all-reduce.1
  93.4 69.1 all-reduce.1
  168.7 69.1 all-reduce.1
  243.6 69.1 all-reduce.1
  318.6 69.1 all-reduce.1
  393.6 69.1 all-reduce.1
  468.9 69.1 all-reduce.1
  544.2 69.1 all-reduce.1
  619.5 69.1 all-reduce.1
  694.5 69.1 all-reduce.1
  769.7 69.1 all-reduce.1
  844.7 69.1 all-reduce.1
  920.0 69.1 all-reduce.1
  995.0 69.1 all-reduce.1
  1070.0 69.1 all-reduce.1
  1144.9 69.1 all-reduce.1
Sparse Core Ops, SparseCore 1:
  1218.3 49.0 all-gather.4
  1269.3 47.7 all-gather.6
  1319.0 47.7 all-gather.8
  1368.8 49.0 all-gather.10
  1422.3 29.5 reduce-scatter.1
where the time goes:
time: 1460 us
  waiting for transfers between devices  1320 us (90%)
  loops' own time  42.1 us (3%)
  local copies, waits for them, and re-layouts  35.6 us (2%)
  matrix products  32.2 us (2%)
  other arithmetic  19.2 us (1%)
  between operations  14.9 us (1%)
    psum x16, waiting for transfers between devices, spread_2(): return lax.psum(jnp.where(mine, value, jnp.zeros_like(value)), axis)  1120 us
    all_gather x1, waiting for transfers between devices, local(): lax.all_gather(key_weight, 'req', axis=0, tiled=True)  45.3 us
    all_gather x1, waiting for transfers between devices, local(): lax.all_gather(query_weight, 'req', axis=0, tiled=True)  44.6 us
    all_gather x1, waiting for transfers between devices, local(): lax.all_gather(value_weight, 'req', axis=0, tiled=True)  43.4 us
    another operation x1, loops' own time, local(): lax.fori_loop(0, active_count, fetch_one, jnp.zeros((active_count,) + sto...  42.1 us
    all_gather x1, waiting for transfers between devices, local(): lax.all_gather(output_weight, 'req', axis=1, tiled=True)  34.4 us
    reduce_scatter x1, waiting for transfers between devices, local(): lax.psum_scatter(partial_out.astype(jnp.bfloat16), 'tp', scatter_dimensio...  29.6 us
  transfers between devices with their start and end apart: 21, of which 21 were waited for; matrix products, arithmetic and copies ran while one was open for 2% of the time, Pallas kernels for 0%

commit v1 on v0

--- a/solution.py
+++ b/solution.py
@@ -103,11 +103,26 @@
         lax.all_gather(query_weight, "req", axis=0, tiled=True),
         preferred_element_type=jnp.float32,
     )
-    key_base = jnp.dot(
-        normed,
-        lax.all_gather(key_weight, "req", axis=0, tiled=True),
-        preferred_element_type=jnp.float32,
-    )
+
+    def define_yards(here_x, group_axis):
+        arr_next = lax.axis_size(group_axis)
+        built, t1, current_block = (arr_next, lax.axis_index(group_axis), here_x.shape[0])
+        all_rows = [m * built if pp == 0 else m for pp, m in enumerate(here_x.shape)]
+        main = lax.dynamic_update_slice_in_dim(
+            jnp.zeros(all_rows, here_x.dtype), here_x, t1 * current_block, axis=0
+        )
+        for src_i in range(1, built):
+            here_x = lax.ppermute(
+                here_x,
+                axis_name=group_axis,
+                perm=list(map(lambda pp: (pp, (pp + 1) % built), range(built))),
+            )
+            main = lax.dynamic_update_slice_in_dim(
+                main, here_x, (t1 - src_i) % built * current_block, axis=0
+            )
+        return main
+
+    key_base = jnp.dot(normed, define_yards(key_weight, "req"), preferred_element_type=jnp.float32)
     value_plain = jnp.dot(
         normed,
         lax.all_gather(value_weight, "req", axis=0, tiled=True),

time: 1460 us -> 1430 us (0.979)
  waiting for transfers between devices: 1320 us -> 1270 us
    ppermute x0 -> x7, waiting for transfers between devices: none -> 72.9 us  [define_yards(): lax.ppermute(here_x, axis_name=group_axis, perm=list(map(lambda pp: (pp,...]
    all_gather x1 -> x0, waiting for transfers between devices: 45.3 us -> none  [local(): lax.all_gather(key_weight, 'req', axis=0, tiled=True)]
    all_gather x1, waiting for transfers between devices: 43.4 us -> 0.01 us  [local(): lax.all_gather(value_weight, 'req', axis=0, tiled=True)]
    all_gather x1, waiting for transfers between devices: 44.6 us -> 16.6 us  [local(): lax.all_gather(query_weight, 'req', axis=0, tiled=True)]
  transfers between devices with their start and end apart: 21 -> 27, of which waited for: 21 -> 26; matrix products, arithmetic and copies ran while one was open for 2% -> 3% of each run, Pallas kernels for 0% -> 0%
where the time goes in v1:
time: 1430 us
  waiting for transfers between devices  1270 us (89%)
  local copies, waits for them, and re-layouts  44.7 us (3%)
  loops' own time  42.1 us (3%)
  matrix products  32.2 us (2%)
  other arithmetic  19.6 us (1%)
  between operations  15 us (1%)
    psum x16, waiting for transfers between devices, spread_2(): return lax.psum(jnp.where(mine, value, jnp.zeros_like(value)), axis)  1120 us
    ppermute x7, waiting for transfers between devices, define_yards(): lax.ppermute(here_x, axis_name=group_axis, perm=list(map(lambda pp: (pp,...  72.9 us
    another operation x1, loops' own time, local(): lax.fori_loop(0, active_count, fetch_one, jnp.zeros((active_count,) + sto...  42.1 us
    all_gather x1, waiting for transfers between devices, local(): lax.all_gather(output_weight, 'req', axis=1, tiled=True)  33.2 us
    reduce_scatter x1, waiting for transfers between devices, local(): lax.psum_scatter(partial_out.astype(jnp.bfloat16), 'tp', scatter_dimensio...  29.6 us
  transfers between devices with their start and end apart: 27, of which 26 were waited for; matrix products, arithmetic and copies ran while one was open for 3% of the time, Pallas kernels for 0%

profile of v1, /device:TPU:0, one launch (start us, length us, event | category | flops | bytes accessed | tf_op | source)
XLA Modules:
  0.0 1425.8 jit_solution(9688842935571006525)
XLA Ops:
  10.6 1205.2 %while.15 = (s32[]{:T(128)}, bf16[16,2,16,2560]{3,2,1,0:T(8,128)(2,1)}, s32[16]{0:T(128)S(1)}, bf16[2,2,16,2560]{3,2,1,0:T(8,128)(2,1)S(1)}, s32[]{:T(128)}, /*i...) while((s32[]{:T(128)}, bf16[16,2,16,2560]{3,2,1,0:T(8,128)(2,1)}, s32[16]{0:T(128)S(1)}, ...), condition=%wide.region_4.5_spmd, body=%wide.region_2.4_spmd.sunk | while | flops 163868 | bytes 1638832 | solution.py:87
  14.5 72.8 %all-reduce.2.cloned.1.call-done = bf16[1,2,16,2560]{3,2,1,0:T(8,128)(2,1)} async-done(((bf16[1,2,16,2560]{3,2,1,0:T(8,128)(2,1)}), bf16[1,2,16,2560]{3,2,1,0:T(8,128)(2,1)}) %all-reduce.2.cloned.1.call-update) | async-done | bytes 163856 | tf_op jit(solution)/shard_map/while/body/eval_jaxpr/psum | solution.py:14
  92.8 69.8 %all-reduce.2.cloned.1.call-done = bf16[1,2,16,2560]{3,2,1,0:T(8,128)(2,1)} async-done(((bf16[1,2,16,2560]{3,2,1,0:T(8,128)(2,1)}), bf16[1,2,16,2560]{3,2,1,0:T(8,128)(2,1)}) %all-reduce.2.cloned.1.call-update) | async-done | bytes 163856 | tf_op jit(solution)/shard_map/while/body/eval_jaxpr/psum | solution.py:14
  162.6 1.6 constant_dynamic-update-slice_fusion.10
  168.1 69.8 %all-reduce.2.cloned.1.call-done = bf16[1,2,16,2560]{3,2,1,0:T(8,128)(2,1)} async-done(((bf16[1,2,16,2560]{3,2,1,0:T(8,128)(2,1)}), bf16[1,2,16,2560]{3,2,1,0:T(8,128)(2,1)}) %all-reduce.2.cloned.1.call-update) | async-done | bytes 163856 | tf_op jit(solution)/shard_map/while/body/eval_jaxpr/psum | solution.py:14
  237.9 1.6 constant_dynamic-update-slice_fusion.10
  243.4 69.5 %all-reduce.2.cloned.1.call-done = bf16[1,2,16,2560]{3,2,1,0:T(8,128)(2,1)} async-done(((bf16[1,2,16,2560]{3,2,1,0:T(8,128)(2,1)}), bf16[1,2,16,2560]{3,2,1,0:T(8,128)(2,1)}) %all-reduce.2.cloned.1.call-update) | async-done | bytes 163856 | tf_op jit(solution)/shard_map/while/body/eval_jaxpr/psum | solution.py:14
  312.9 1.6 constant_dynamic-update-slice_fusion.10
  318.4 69.5 %all-reduce.2.cloned.1.call-done = bf16[1,2,16,2560]{3,2,1,0:T(8,128)(2,1)} async-done(((bf16[1,2,16,2560]{3,2,1,0:T(8,128)(2,1)}), bf16[1,2,16,2560]{3,2,1,0:T(8,128)(2,1)}) %all-reduce.2.cloned.1.call-update) | async-done | bytes 163856 | tf_op jit(solution)/shard_map/while/body/eval_jaxpr/psum | solution.py:14
  387.8 1.6 constant_dynamic-update-slice_fusion.10
  393.3 69.5 %all-reduce.2.cloned.1.call-done = bf16[1,2,16,2560]{3,2,1,0:T(8,128)(2,1)} async-done(((bf16[1,2,16,2560]{3,2,1,0:T(8,128)(2,1)}), bf16[1,2,16,2560]{3,2,1,0:T(8,128)(2,1)}) %all-reduce.2.cloned.1.call-update) | async-done | bytes 163856 | tf_op jit(solution)/shard_map/while/body/eval_jaxpr/psum | solution.py:14
  462.8 1.6 constant_dynamic-update-slice_fusion.10
  468.3 69.8 %all-reduce.2.cloned.1.call-done = bf16[1,2,16,2560]{3,2,1,0:T(8,128)(2,1)} async-done(((bf16[1,2,16,2560]{3,2,1,0:T(8,128)(2,1)}), bf16[1,2,16,2560]{3,2,1,0:T(8,128)(2,1)}) %all-reduce.2.cloned.1.call-update) | async-done | bytes 163856 | tf_op jit(solution)/shard_map/while/body/eval_jaxpr/psum | solution.py:14
  543.6 69.8 %all-reduce.2.cloned.1.call-done = bf16[1,2,16,2560]{3,2,1,0:T(8,128)(2,1)} async-done(((bf16[1,2,16,2560]{3,2,1,0:T(8,128)(2,1)}), bf16[1,2,16,2560]{3,2,1,0:T(8,128)(2,1)}) %all-reduce.2.cloned.1.call-update) | async-done | bytes 163856 | tf_op jit(solution)/shard_map/while/body/eval_jaxpr/psum | solution.py:14
  613.4 1.6 constant_dynamic-update-slice_fusion.10
  618.9 69.8 %all-reduce.2.cloned.1.call-done = bf16[1,2,16,2560]{3,2,1,0:T(8,128)(2,1)} async-done(((bf16[1,2,16,2560]{3,2,1,0:T(8,128)(2,1)}), bf16[1,2,16,2560]{3,2,1,0:T(8,128)(2,1)}) %all-reduce.2.cloned.1.call-update) | async-done | bytes 163856 | tf_op jit(solution)/shard_map/while/body/eval_jaxpr/psum | solution.py:14
  688.7 1.6 constant_dynamic-update-slice_fusion.10
  694.2 69.5 %all-reduce.2.cloned.1.call-done = bf16[1,2,16,2560]{3,2,1,0:T(8,128)(2,1)} async-done(((bf16[1,2,16,2560]{3,2,1,0:T(8,128)(2,1)}), bf16[1,2,16,2560]{3,2,1,0:T(8,128)(2,1)}) %all-reduce.2.cloned.1.call-update) | async-done | bytes 163856 | tf_op jit(solution)/shard_map/while/body/eval_jaxpr/psum | solution.py:14
  769.2 69.8 %all-reduce.2.cloned.1.call-done = bf16[1,2,16,2560]{3,2,1,0:T(8,128)(2,1)} async-done(((bf16[1,2,16,2560]{3,2,1,0:T(8,128)(2,1)}), bf16[1,2,16,2560]{3,2,1,0:T(8,128)(2,1)}) %all-reduce.2.cloned.1.call-update) | async-done | bytes 163856 | tf_op jit(solution)/shard_map/while/body/eval_jaxpr/psum | solution.py:14
  838.9 1.6 constant_dynamic-update-slice_fusion.10
  844.4 69.5 %all-reduce.2.cloned.1.call-done = bf16[1,2,16,2560]{3,2,1,0:T(8,128)(2,1)} async-done(((bf16[1,2,16,2560]{3,2,1,0:T(8,128)(2,1)}), bf16[1,2,16,2560]{3,2,1,0:T(8,128)(2,1)}) %all-reduce.2.cloned.1.call-update) | async-done | bytes 163856 | tf_op jit(solution)/shard_map/while/body/eval_jaxpr/psum | solution.py:14
  913.9 1.6 constant_dynamic-update-slice_fusion.10
  919.4 69.8 %all-reduce.2.cloned.1.call-done = bf16[1,2,16,2560]{3,2,1,0:T(8,128)(2,1)} async-done(((bf16[1,2,16,2560]{3,2,1,0:T(8,128)(2,1)}), bf16[1,2,16,2560]{3,2,1,0:T(8,128)(2,1)}) %all-reduce.2.cloned.1.call-update) | async-done | bytes 163856 | tf_op jit(solution)/shard_map/while/body/eval_jaxpr/psum | solution.py:14
  994.7 69.5 %all-reduce.2.cloned.1.call-done = bf16[1,2,16,2560]{3,2,1,0:T(8,128)(2,1)} async-done(((bf16[1,2,16,2560]{3,2,1,0:T(8,128)(2,1)}), bf16[1,2,16,2560]{3,2,1,0:T(8,128)(2,1)}) %all-reduce.2.cloned.1.call-update) | async-done | bytes 163856 | tf_op jit(solution)/shard_map/while/body/eval_jaxpr/psum | solution.py:14
  1064.2 1.6 constant_dynamic-update-slice_fusion.10
  1069.7 69.5 %all-reduce.2.cloned.1.call-done = bf16[1,2,16,2560]{3,2,1,0:T(8,128)(2,1)} async-done(((bf16[1,2,16,2560]{3,2,1,0:T(8,128)(2,1)}), bf16[1,2,16,2560]{3,2,1,0:T(8,128)(2,1)}) %all-reduce.2.cloned.1.call-update) | async-done | bytes 163856 | tf_op jit(solution)/shard_map/while/body/eval_jaxpr/psum | solution.py:14
  1144.6 69.5 %all-reduce.2.cloned.1.call-done = bf16[1,2,16,2560]{3,2,1,0:T(8,128)(2,1)} async-done(((bf16[1,2,16,2560]{3,2,1,0:T(8,128)(2,1)}), bf16[1,2,16,2560]{3,2,1,0:T(8,128)(2,1)}) %all-reduce.2.cloned.1.call-update) | async-done | bytes 163856 | tf_op jit(solution)/shard_map/while/body/eval_jaxpr/psum | solution.py:14
  1214.1 1.6 constant_dynamic-update-slice_fusion.10
  1219.0 3.0 fusion.23
  1221.9 4.1 collective-permute-done
  1226.8 14.9 %collective-permute-done.1 = bf16[256,512]{1,0:T(8,128)(2,1)S(1)} collective-permute-done((bf16[256,512]{1,0:T(8,128)(2,1)S(1)}, bf16[256,512]{1,0:T(8,128)(2,1)S(1)}, u32[]{:S(2)}, u32[]{:S(2)}) %collective-permute-start.1) | collective-permute-done | bytes 262176 | tf_op jit(solution)/shard_map/ppermute | solution.py:115
  1241.8 9.0 collective-permute-done.2
  1252.7 14.8 %collective-permute-done.3 = bf16[256,512]{1,0:T(8,128)(2,1)} collective-permute-done((bf16[256,512]{1,0:T(8,128)(2,1)S(1)}, bf16[256,512]{1,0:T(8,128)(2,1)}, u32[]{:S(2)}, u32[]{:S(2)}) %collective-permute-start.3) | collective-permute-done | bytes 262176 | tf_op jit(solution)/shard_map/ppermute | solution.py:115
  1269.7 13.0 collective-permute-done.4
  1284.9 9.0 collective-permute-done.5
  1293.9 1.7 constant_dynamic-update-slice_fusion.4
  1295.6 1.7 constant_dynamic-update-slice_fusion.3
  1298.0 8.0 collective-permute-done.6
  1306.7 4.0 fusion.39
  1310.7 3.0 fusion.44
  1315.1 16.6 %all-gather.6.cloned.1.call-done = bf16[2048,512]{1,0:T(8,128)(2,1)} async-done(((bf16[256,512]{1,0:T(8,128)(2,1)}), bf16[2048,512]{1,0:T(8,128)(2,1)}) %all-gather.6.cloned.1.call-update) | async-done | bytes 2097168 | tf_op jit(solution)/shard_map/all_gather | solution.py:103
  1331.6 3.0 fusion.41
  1337.2 7.9 fusion.46
  1345.1 4.3 fusion.21
  1349.4 33.2 %all-gather.8.cloned.1.call-done = bf16[512,2048]{1,0:T(8,128)(2,1)} async-done(((bf16[512,256]{1,0:T(8,128)(2,1)}), bf16[512,2048]{1,0:T(8,128)(2,1)}) %all-gather.8.cloned.1.call-update) | async-done | bytes 2097168 | tf_op jit(solution)/shard_map/all_gather | solution.py:178
  1382.6 4.2 convolution_convert_fusion
  1386.8 29.6 %reduce-scatter.2.cloned.1.call-done = bf16[512,512]{1,0:T(8,128)(2,1)} async-done(((bf16[512,2048]{1,0:T(8,128)(2,1)}), bf16[512,512]{1,0:T(8,128)(2,1)}) %reduce-scatter.2.cloned.1.call-update) | async-done | bytes 524304 | tf_op jit(solution)/shard_map/reduce_scatter | solution.py:181
  1416.4 2.0 add_convert_fusion
  (133 shorter events, 47.1 us)
Async XLA Ops:
  7.4 0.7 copy-start
  8.1 1208.9 %copy-start.3 = (bf16[256,512]{1,0:T(8,128)(2,1)S(1)}, bf16[256,512]{1,0:T(8,128)(2,1)}, u32[]{:S(2)}) copy-start(bf16[256,512]{1,0:T(8,128)(2,1)} %param.21) | copy-start | bytes 786436
  9.4 1209.0 %copy-start.1 = (bf16[512,2048]{1,0:T(8,128)(2,1)S(1)}, bf16[512,2048]{1,0:T(8,128)(2,1)}, u32[]{:S(2)}) copy-start(bf16[512,2048]{1,0:T(8,128)(2,1)} %param.14) | copy-start | bytes 6291460
  10.6 1207.8 %copy-start.6 = (bf16[2048]{0:T(1024)(128)(2,1)S(1)}, bf16[2048]{0:T(1024)(128)(2,1)}, u32[]{:S(2)}) copy-start(bf16[2048]{0:T(1024)(128)(2,1)} %param.19) | copy-start | bytes 12292
  10.6 76.7 %all-reduce.2.cloned.1.call-start = ((), (), s32[]{:S(2)}) async-start(), calls=%async_computation.5 | async-start | bytes 327680 | tf_op jit(solution)/shard_map/while/body/eval_jaxpr/psum | solution.py:14
  88.9 73.7 %all-reduce.2.cloned.1.call-start = ((), (), s32[]{:S(2)}) async-start(), calls=%async_computation.5 | async-start | bytes 327680 | tf_op jit(solution)/shard_map/while/body/eval_jaxpr/psum | solution.py:14
  164.2 73.7 %all-reduce.2.cloned.1.call-start = ((), (), s32[]{:S(2)}) async-start(), calls=%async_computation.5 | async-start | bytes 327680 | tf_op jit(solution)/shard_map/while/body/eval_jaxpr/psum | solution.py:14
  239.5 73.4 %all-reduce.2.cloned.1.call-start = ((), (), s32[]{:S(2)}) async-start(), calls=%async_computation.5 | async-start | bytes 327680 | tf_op jit(solution)/shard_map/while/body/eval_jaxpr/psum | solution.py:14
  314.5 73.4 %all-reduce.2.cloned.1.call-start = ((), (), s32[]{:S(2)}) async-start(), calls=%async_computation.5 | async-start | bytes 327680 | tf_op jit(solution)/shard_map/while/body/eval_jaxpr/psum | solution.py:14
  389.4 73.4 %all-reduce.2.cloned.1.call-start = ((), (), s32[]{:S(2)}) async-start(), calls=%async_computation.5 | async-start | bytes 327680 | tf_op jit(solution)/shard_map/while/body/eval_jaxpr/psum | solution.py:14
  464.4 73.7 %all-reduce.2.cloned.1.call-start = ((), (), s32[]{:S(2)}) async-start(), calls=%async_computation.5 | async-start | bytes 327680 | tf_op jit(solution)/shard_map/while/body/eval_jaxpr/psum | solution.py:14
  539.7 73.7 %all-reduce.2.cloned.1.call-start = ((), (), s32[]{:S(2)}) async-start(), calls=%async_computation.5 | async-start | bytes 327680 | tf_op jit(solution)/shard_map/while/body/eval_jaxpr/psum | solution.py:14
  615.0 73.7 %all-reduce.2.cloned.1.call-start = ((), (), s32[]{:S(2)}) async-start(), calls=%async_computation.5 | async-start | bytes 327680 | tf_op jit(solution)/shard_map/while/body/eval_jaxpr/psum | solution.py:14
  690.3 73.4 %all-reduce.2.cloned.1.call-start = ((), (), s32[]{:S(2)}) async-start(), calls=%async_computation.5 | async-start | bytes 327680 | tf_op jit(solution)/shard_map/while/body/eval_jaxpr/psum | solution.py:14
  765.2 73.7 %all-reduce.2.cloned.1.call-start = ((), (), s32[]{:S(2)}) async-start(), calls=%async_computation.5 | async-start | bytes 327680 | tf_op jit(solution)/shard_map/while/body/eval_jaxpr/psum | solution.py:14
  840.5 73.4 %all-reduce.2.cloned.1.call-start = ((), (), s32[]{:S(2)}) async-start(), calls=%async_computation.5 | async-start | bytes 327680 | tf_op jit(solution)/shard_map/while/body/eval_jaxpr/psum | solution.py:14
  915.5 73.7 %all-reduce.2.cloned.1.call-start = ((), (), s32[]{:S(2)}) async-start(), calls=%async_computation.5 | async-start | bytes 327680 | tf_op jit(solution)/shard_map/while/body/eval_jaxpr/psum | solution.py:14
  990.8 73.4 %all-reduce.2.cloned.1.call-start = ((), (), s32[]{:S(2)}) async-start(), calls=%async_computation.5 | async-start | bytes 327680 | tf_op jit(solution)/shard_map/while/body/eval_jaxpr/psum | solution.py:14
  1065.8 73.4 %all-reduce.2.cloned.1.call-start = ((), (), s32[]{:S(2)}) async-start(), calls=%async_computation.5 | async-start | bytes 327680 | tf_op jit(solution)/shard_map/while/body/eval_jaxpr/psum | solution.py:14
  1140.7 73.4 %all-reduce.2.cloned.1.call-start = ((), (), s32[]{:S(2)}) async-start(), calls=%async_computation.5 | async-start | bytes 327680 | tf_op jit(solution)/shard_map/while/body/eval_jaxpr/psum | solution.py:14
  1215.7 3.1 copy-start.5
  1215.7 3.1 copy-start.7
  1215.7 95.0 %all-gather.4.cloned.1.call-start = ((), (), s32[]{:S(2)}) async-start(), calls=%async_computation.1 | async-start | bytes 2359296 | tf_op jit(solution)/shard_map/all_gather | solution.py:128
  1216.3 115.3 %all-gather.6.cloned.1.call-start = ((), (), s32[]{:S(2)}) async-start(), calls=%async_computation.2 | async-start | bytes 2359296 | tf_op jit(solution)/shard_map/all_gather | solution.py:103
  1216.9 165.7 %all-gather.8.cloned.1.call-start = ((), (), s32[]{:S(2)}) async-start(), calls=%async_computation.3 | async-start | bytes 2359296 | tf_op jit(solution)/shard_map/all_gather | solution.py:178
  1217.0 9.1 collective-permute-start
  1218.3 198.2 %reduce-scatter.2.cloned.1.call-start = ((), (), s32[]{:S(2)}) async-start(), calls=%async_computation.4 | async-start | bytes 2621440 | tf_op jit(solution)/shard_map/reduce_scatter | solution.py:181
  1226.1 15.6 %collective-permute-start.1 = (bf16[256,512]{1,0:T(8,128)(2,1)S(1)}, bf16[256,512]{1,0:T(8,128)(2,1)S(1)}, u32[]{:S(2)}, u32[]{:S(2)}) collective-permute-start(bf16[256,512]{1,0:T(8,128)(2,1)S(1)} %collective-permute-done), channel_id=1, source_target_pairs={{0,4},{4,8},{8,12},{12,16},{16,20},{20,24},{24,28},{28,0},{1,5},{5... | collective-permute-start | bytes 786440 | tf_op jit(solution)/shard_map/ppermute | solution.py:115
  1241.7 9.1 collective-permute-start.2
  1250.8 16.7 %collective-permute-start.3 = (bf16[256,512]{1,0:T(8,128)(2,1)S(1)}, bf16[256,512]{1,0:T(8,128)(2,1)}, u32[]{:S(2)}, u32[]{:S(2)}) collective-permute-start(bf16[256,512]{1,0:T(8,128)(2,1)S(1)} %collective-permute-done.2), channel_id=1, source_target_pairs={{0,4},{4,8},{8,12},{12,16},{16,20},{20,24},{24,28},{28,0},{1,5},{5... | collective-permute-start | bytes 786440 | tf_op jit(solution)/shard_map/ppermute | solution.py:115
  1267.5 15.2 %collective-permute-start.4 = (bf16[256,512]{1,0:T(8,128)(2,1)}, bf16[256,512]{1,0:T(8,128)(2,1)}, u32[]{:S(2)}, u32[]{:S(2)}) collective-permute-start(bf16[256,512]{1,0:T(8,128)(2,1)} %collective-permute-done.3), channel_id=1, source_target_pairs={{0,4},{4,8},{8,12},{12,16},{16,20},{20,24},{24,28},{28,0},{1,5},{5... | collective-permute-start | bytes 786440 | tf_op jit(solution)/shard_map/ppermute | solution.py:115
  1282.7 11.2 collective-permute-start.5
  1293.9 12.1 collective-permute-start.6
  1334.6 1.4 copy-start.2
  1334.7 1.4 copy-start.4
Sparse Core Ops, SparseCore 0:
  15.1 72.1 all-reduce.1
  93.4 69.1 all-reduce.1
  168.7 69.1 all-reduce.1
  243.7 69.1 all-reduce.1
  318.7 69.1 all-reduce.1
  393.6 69.1 all-reduce.1
  469.0 69.1 all-reduce.1
  544.2 69.1 all-reduce.1
  619.5 69.1 all-reduce.1
  694.5 69.1 all-reduce.1
  769.8 69.1 all-reduce.1
  844.7 69.1 all-reduce.1
  920.0 69.1 all-reduce.1
  995.0 69.1 all-reduce.1
  1070.0 69.1 all-reduce.1
  1144.9 69.1 all-reduce.1
Sparse Core Ops, SparseCore 1:
  1218.3 58.7 all-gather.3
  1279.0 52.5 all-gather.5
  1333.5 49.0 all-gather.7
  1386.9 29.5 reduce-scatter.1
